TPU v7x, 32 devices: a whole 2x2x4 slice. The times are simulated.
32 devices in a mesh: row: 8 (over y, x, core), col: 4 (over z).
Axes of the slice: x: 2, y: 2, z: 4, core: 2. Of those that a mesh axis runs over, the one named last changes fastest.
Arguments:
- sub_basis: bfloat16 [32, 768, 768], P(('row', 'col')), may hold values from -0.15625 to 0.15625
- coupling: bfloat16 [32, 2, 768, 768], P(('row', 'col')), may hold values from -0.15625 to 0.15625
- pair_live: int32 [32, 2], P(('row', 'col')), may hold values 0 or 1
- offsets: int32 [32], P(('row', 'col')), may hold values from 0 to 3328
- dual_in: float32 [4, 4096], P('col', 'row'), may hold values from -6 to 6
Outputs:
- dual_out: float32 [4, 4096], P('col', 'row')
Inputs may be any that keep to these rules, and one draw needn't show every extreme that they name: `offsets`: each subdomain's window of 768 multipliers lies inside its block column's vector.
All inputs are finite; a program needn't handle non-finite values. No bound on the sum of `pair_live` on one device may be relied on, other than what follows from the above.
Results may differ from a plain program's by a relative error of at most 0.0085.
Values may be sent and summed in bfloat16 or wider, within the bound.
A program may use at most 64 MiB of HBM per device.

v0:
```python
import jax
import jax.numpy as jnp
from jax import lax
from jax.sharding import PartitionSpec as P

W = 768


def passed_along(array, axis, by):
    count = lax.axis_size(axis)
    return lax.ppermute(array, axis, [(i, (i + by) % count) for i in range(count)])


def collect(shard_piece):
    return lax.all_gather(shard_piece, "row", axis=1, tiled=True)


def assemble(partial_value):
    return lax.psum_scatter(partial_value, "row", scatter_dimension=1, tiled=True)


def place(totals, window_start, length):
    zeroed = jnp.zeros((length,), jnp.float32)
    return lax.dynamic_update_slice(zeroed, totals, (window_start,))[None, :]


def split_three(vector):
    high = vector.astype(jnp.bfloat16)
    rest = vector - high.astype(jnp.float32)
    middle = rest.astype(jnp.bfloat16)
    lowest = (rest - middle.astype(jnp.float32)).astype(jnp.bfloat16)
    return jnp.stack([high, middle, lowest], axis=0)


def left_apply(matrix, vector):
    pieces = split_three(vector)
    products = lax.dot_general(
        matrix, pieces, (((1,), (1,)), ((), ())), preferred_element_type=jnp.float32
    )
    return jnp.sum(products, axis=1)


def right_apply(vector, matrix):
    pieces = split_three(vector)
    products = jnp.dot(pieces, matrix, preferred_element_type=jnp.float32)
    return jnp.sum(products, axis=0)


def apply_dual(window, basis_one, own_blocks, mirrored):
    projected = left_apply(basis_one, window)
    summed = right_apply(projected, basis_one)
    for slot_index in range(len(own_blocks)):
        distance = slot_index + 1
        next_dual = passed_along(window, "col", -distance)
        summed = summed + left_apply(own_blocks[slot_index], next_dual)
        behind = passed_along(window, "col", distance)
        summed = summed + right_apply(behind, mirrored[slot_index])
    return summed


def on_device(sub_basis, coupling, pair_live, offsets, dual_in):
    basis_one = sub_basis[0]
    blocks = []
    for slot_index in range(coupling.shape[1]):
        coupling_one = coupling[0, slot_index]

        def form_block(operand, coupling_one=coupling_one):
            return jnp.einsum(
                "kv,kw->vw", basis_one, coupling_one, preferred_element_type=jnp.float32
            ).astype(jnp.bfloat16)

        def skip_block(operand):
            return jnp.zeros((W, W), jnp.bfloat16)

        blocks.append(lax.cond(pair_live[0, slot_index] > 0, form_block, skip_block, 0))
    mirrored = []
    for slot_index in range(len(blocks)):
        mirrored.append(passed_along(blocks[slot_index], "col", slot_index + 1))
    dual_len = dual_in.shape[1] * lax.axis_size("row")
    window_start = offsets[0]
    column_vec = collect(dual_in)[0]
    window = lax.dynamic_slice_in_dim(column_vec, window_start, W)
    first_local = apply_dual(window, basis_one, blocks, mirrored)
    partial_value = place(first_local, window_start, dual_len)
    column_vec = collect(assemble(partial_value))[0]
    window = lax.dynamic_slice_in_dim(column_vec, window_start, W)
    second_local = apply_dual(window, basis_one, blocks, mirrored)
    return assemble(place(second_local, window_start, dual_len))


def solution(mesh):
    return jax.shard_map(
        on_device,
        mesh=mesh,
        in_specs=(
            P(("row", "col"), None, None),
            P(("row", "col"), None, None, None),
            P(("row", "col"), None),
            P(("row", "col")),
            P("col", "row"),
        ),
        out_specs=P("col", "row"),
        check_vma=False,
    )
```

profile of v0, /device:TPU:0, one launch (start us, length us, event | category | flops | bytes accessed | tf_op | source)
XLA Modules:
  0.0 227.0 jit_solution(14171642045918403011)
XLA Ops:
  7.2 10.5 %all_gather.6 = f32[1,4096]{1,0:T(1,128)S(1)} all-gather(f32[1,512]{1,0:T(1,128)} %param.13), channel_id=1, replica_groups=mesh['row'=8,'col'=4] {'row'}, dimensions={1}, use_global_device_ids=true | all-gather | bytes 18432 | tf_op jit(solution)/shard_map/all_gather | solution.py:15
  17.7 1.3 fusion.50
  18.9 2.6 %collective-permute-start.3 = (f32[768]{0:T(1024)}, f32[768]{0:T(1024)}, u32[]{:S(2)}, u32[]{:S(2)}) collective-permute-start(f32[768]{0:T(1024)} %get-tuple-element.31), channel_id=1, source_target_pairs={{0,2},{1,3},{2,0},{3,1},{4,6},{5,7},{6,4},{7,5},{8,10},{9,11},{10,... | collective-permute-start | bytes 9224 | tf_op jit(solution)/shard_map/ppermute | solution.py:11
  21.5 1.6 collective-permute-start.1
  23.1 2.2 collective-permute-start
  25.4 1.3 fusion.76
  28.2 5.2 %collective-permute-start.2 = (bf16[768,768]{1,0:T(8,128)(2,1)S(1)}, bf16[768,768]{1,0:T(8,128)(2,1)S(1)}, u32[]{:S(2)}, u32[]{:S(2)}) collective-permute-start(bf16[768,768]{1,0:T(8,128)(2,1)S(1)} %get-tuple-element.57), channel_id=1, source_target_pairs={{0,1},{1,2},{2,3},{3,0},{4,5},{5,6},{6,7},{7,4},{8,9},{9,10},{10,1... | collective-permute-start | bytes 3538952 | tf_op jit(solution)/shard_map/ppermute | solution.py:11
  33.4 1.7 convolution_reduce_fusion.11
  36.3 0.8 fusion.74
  38.8 68.5 %collective-permute-done.4 = bf16[768,768]{1,0:T(8,128)(2,1)} collective-permute-done((bf16[768,768]{1,0:T(8,128)(2,1)S(1)}, bf16[768,768]{1,0:T(8,128)(2,1)}, u32[]{:S(2)}, u32[]{:S(2)}) %collective-permute-start.4) | collective-permute-done | bytes 1179680 | tf_op jit(solution)/shard_map/ppermute | solution.py:11
  107.3 1.6 convolution_reduce_fusion.6
  108.9 1.0 copy-done.1
  110.8 1.0 dynamic_update_slice.8
  111.8 2.0 copy.6
  113.9 38.5 %reduce-scatter.7.cloned.1.call-done = f32[512,1]{1,0:T(8,128)} async-done(((f32[4096,1]{1,0:T(8,128)}), f32[512,1]{1,0:T(8,128)}) %reduce-scatter.7.cloned.1.call-update) | async-done | bytes 2064
  152.3 1.6 copy.7
  154.0 8.8 %all_gather.7 = f32[1,4096]{1,0:T(1,128)S(1)} all-gather(f32[1,512]{1,0:T(1,128)} %copy.7), channel_id=1, replica_groups=mesh['row'=8,'col'=4] {'row'}, dimensions={1}, use_global_device_ids=true | all-gather | bytes 18432 | tf_op jit(solution)/shard_map/all_gather | solution.py:15
  163.5 3.4 %collective-permute-start.5 = (f32[768]{0:T(1024)S(1)}, f32[768]{0:T(1024)S(1)}, u32[]{:S(2)}, u32[]{:S(2)}) collective-permute-start(f32[768]{0:T(1024)S(1)} %get-tuple-element.28), channel_id=1, source_target_pairs={{0,3},{1,0},{2,1},{3,2},{4,7},{5,4},{6,5},{7,6},{8,11},{9,8},{10,9... | collective-permute-start | bytes 9224 | tf_op jit(solution)/shard_map/ppermute | solution.py:11
  166.8 1.1 collective-permute-start.7
  168.3 4.0 %collective-permute-done.6 = f32[768]{0:T(1024)S(1)} collective-permute-done((f32[768]{0:T(1024)S(1)}, f32[768]{0:T(1024)S(1)}, u32[]{:S(2)}, u32[]{:S(2)}) %collective-permute-start.6) | collective-permute-done | bytes 3104 | tf_op jit(solution)/shard_map/ppermute | solution.py:11
  173.3 1.6 convolution_reduce_fusion
  175.6 2.0 copy.8
  177.6 40.9 %reduce-scatter.9.cloned.1.call-done = f32[512,1]{1,0:T(8,128)} async-done(((f32[4096,1]{1,0:T(8,128)}), f32[512,1]{1,0:T(8,128)}) %reduce-scatter.9.cloned.1.call-update) | async-done | bytes 2064
  218.5 1.6 copy.9
  (67 shorter events, 6.7 us)
Async XLA Ops:
  6.5 145.8 %reduce-scatter.7.cloned.1.call-start = ((), (), s32[]{:S(2)}) async-start(), calls=%async_computation.2 | async-start | bytes 2359296
  18.9 16.6 %collective-permute-start.3 = (f32[768]{0:T(1024)}, f32[768]{0:T(1024)}, u32[]{:S(2)}, u32[]{:S(2)}) collective-permute-start(f32[768]{0:T(1024)} %get-tuple-element.31), channel_id=1, source_target_pairs={{0,2},{1,3},{2,0},{3,1},{4,6},{5,7},{6,4},{7,5},{8,10},{9,11},{10,... | collective-permute-start | bytes 9224 | tf_op jit(solution)/shard_map/ppermute | solution.py:11
  21.5 14.7 %collective-permute-start.1 = (f32[768]{0:T(1024)}, f32[768]{0:T(1024)}, u32[]{:S(2)}, u32[]{:S(2)}) collective-permute-start(f32[768]{0:T(1024)} %get-tuple-element.31), channel_id=1, source_target_pairs={{0,1},{1,2},{2,3},{3,0},{4,5},{5,6},{6,7},{7,4},{8,9},{9,10},{10,1... | collective-permute-start | bytes 9224 | tf_op jit(solution)/shard_map/ppermute | solution.py:11
  23.1 14.0 %collective-permute-start = (f32[768]{0:T(1024)}, f32[768]{0:T(1024)}, u32[]{:S(2)}, u32[]{:S(2)}) collective-permute-start(f32[768]{0:T(1024)} %get-tuple-element.31), channel_id=1, source_target_pairs={{0,3},{1,0},{2,1},{3,2},{4,7},{5,4},{6,5},{7,6},{8,11},{9,8},{10,9... | collective-permute-start | bytes 9224 | tf_op jit(solution)/shard_map/ppermute | solution.py:11
  27.3 80.0 %collective-permute-start.4 = (bf16[768,768]{1,0:T(8,128)(2,1)S(1)}, bf16[768,768]{1,0:T(8,128)(2,1)}, u32[]{:S(2)}, u32[]{:S(2)}) collective-permute-start(bf16[768,768]{1,0:T(8,128)(2,1)S(1)} %get-tuple-element.58), channel_id=1, source_target_pairs={{0,2},{1,3},{2,0},{3,1},{4,6},{5,7},{6,4},{7,5},{8,10},{9,11},{10,... | collective-permute-start | bytes 3538952 | tf_op jit(solution)/shard_map/ppermute | solution.py:11
  28.2 7.0 %copy-start = (bf16[1,768,768]{2,1,0:T(8,128)(2,1)S(1)}, bf16[1,768,768]{2,1,0:T(8,128)(2,1)}, u32[]{:S(2)}) copy-start(bf16[1,768,768]{2,1,0:T(8,128)(2,1)} %param.9) | copy-start | bytes 3538948
  28.2 80.7 %collective-permute-start.2 = (bf16[768,768]{1,0:T(8,128)(2,1)S(1)}, bf16[768,768]{1,0:T(8,128)(2,1)S(1)}, u32[]{:S(2)}, u32[]{:S(2)}) collective-permute-start(bf16[768,768]{1,0:T(8,128)(2,1)S(1)} %get-tuple-element.57), channel_id=1, source_target_pairs={{0,1},{1,2},{2,3},{3,0},{4,5},{5,6},{6,7},{7,4},{8,9},{9,10},{10,1... | collective-permute-start | bytes 3538952 | tf_op jit(solution)/shard_map/ppermute | solution.py:11
  108.9 1.0 copy-start.1
  113.8 104.7 %reduce-scatter.9.cloned.1.call-start = ((), (), s32[]{:S(2)}) async-start(), calls=%async_computation.3 | async-start | bytes 2359296
  163.5 4.8 %collective-permute-start.5 = (f32[768]{0:T(1024)S(1)}, f32[768]{0:T(1024)S(1)}, u32[]{:S(2)}, u32[]{:S(2)}) collective-permute-start(f32[768]{0:T(1024)S(1)} %get-tuple-element.28), channel_id=1, source_target_pairs={{0,3},{1,0},{2,1},{3,2},{4,7},{5,4},{6,5},{7,6},{8,11},{9,8},{10,9... | collective-permute-start | bytes 9224 | tf_op jit(solution)/shard_map/ppermute | solution.py:11
  166.8 5.4 %collective-permute-start.6 = (f32[768]{0:T(1024)S(1)}, f32[768]{0:T(1024)S(1)}, u32[]{:S(2)}, u32[]{:S(2)}) collective-permute-start(f32[768]{0:T(1024)S(1)} %get-tuple-element.28), channel_id=1, source_target_pairs={{0,1},{1,2},{2,3},{3,0},{4,5},{5,6},{6,7},{7,4},{8,9},{9,10},{10,1... | collective-permute-start | bytes 9224 | tf_op jit(solution)/shard_map/ppermute | solution.py:11
  166.8 5.5 %collective-permute-start.7 = (f32[768]{0:T(1024)S(1)}, f32[768]{0:T(1024)S(1)}, u32[]{:S(2)}, u32[]{:S(2)}) collective-permute-start(f32[768]{0:T(1024)S(1)} %get-tuple-element.28), channel_id=1, source_target_pairs={{0,2},{1,3},{2,0},{3,1},{4,6},{5,7},{6,4},{7,5},{8,10},{9,11},{10,... | collective-permute-start | bytes 9224 | tf_op jit(solution)/shard_map/ppermute | solution.py:11
  172.8 2.0 copy-start.2
Sparse Core Ops, SparseCore 0:
  113.9 38.3 reduce-scatter.6
  177.7 40.7 reduce-scatter.8
where the time goes:
time: 228 us; the launch traced here: 227 us
  waiting for transfers between devices  152 us (67%)
  blocking collectives  19.3 us (8%)
  starting transfers between devices  16.2 us (7%)
  between operations  15.8 us (7%)
  local copies, waits for them, and re-layouts  12 us (5%)
  matrix products  8.15 us (4%)
  other arithmetic  3.68 us (2%)
    unnamed x4, waiting for transfers between devices  79.4 us
    ppermute x8, waiting for transfers between devices, passed_along(): lax.ppermute(array, axis, [(i, (i + by) % count) for i in range(count)])  72.5 us
    all_gather x2, blocking collectives, collect(): return lax.all_gather(shard_piece, 'row', axis=1, tiled=True)  19.3 us
    ppermute x8, starting transfers between devices, passed_along(): lax.ppermute(array, axis, [(i, (i + by) % count) for i in range(count)])  16.1 us
    unnamed x10, local copies, waits for them, and re-layouts  8.33 us
  transfers between devices with their start and end apart: 10, of which 4 were waited for; matrix products, arithmetic and copies ran while one was open for 4% of the time, Pallas kernels for 0%

commit v1 on v0

v1 whole, which is shorter than its diff:
```python
import jax
import jax.numpy as jnp
from jax import lax
from jax.sharding import PartitionSpec as P


def passed_along(array, axis, by):
    count = lax.axis_size(axis)
    return lax.ppermute(array, axis, [(i, (i + by) % count) for i in range(count)])


def left_apply(matrix, vector):
    return lax.dot_general(
        matrix, vector, (((1,), (0,)), ((), ())),
        precision=lax.Precision.HIGHEST, preferred_element_type=jnp.float32,
    )


def right_apply(vector, matrix):
    return jnp.dot(vector, matrix, precision=lax.Precision.HIGHEST, preferred_element_type=jnp.float32)


def apply_dual(window, basis, couplings, live):
    projected = left_apply(basis, window)
    inner = projected
    summed = jnp.zeros_like(window)
    for slot, coupling in enumerate(couplings):
        distance = slot + 1
        ahead = passed_along(window, "col", -distance)
        inner = inner + live[slot] * left_apply(coupling, ahead)
        back = live[slot] * right_apply(projected, coupling)
        summed = summed + passed_along(back, "col", distance)
    return summed + right_apply(inner, basis)


def on_device(sub_basis, coupling, pair_live, offsets, dual_in):
    width = sub_basis.shape[2]
    basis = sub_basis[0].astype(jnp.float32)
    couplings = [coupling[0, h].astype(jnp.float32) for h in range(coupling.shape[1])]
    live = pair_live[0].astype(jnp.float32)
    length = dual_in.shape[1] * lax.axis_size("row")
    start = offsets[0]
    piece = dual_in
    for _ in range(2):
        column = lax.all_gather(piece, "row", axis=1, tiled=True)[0]
        window = lax.dynamic_slice_in_dim(column, start, width)
        local = apply_dual(window, basis, couplings, live)
        placed = lax.dynamic_update_slice(jnp.zeros((length,), jnp.float32), local, (start,))
        piece = lax.psum_scatter(placed[None, :], "row", scatter_dimension=1, tiled=True)
    return piece


def solution(mesh):
    return jax.shard_map(
        on_device,
        mesh=mesh,
        in_specs=(
            P(("row", "col"), None, None),
            P(("row", "col"), None, None, None),
            P(("row", "col"), None),
            P(("row", "col")),
            P("col", "row"),
        ),
        out_specs=P("col", "row"),
        check_vma=False,
    )
```

time: 228 us -> 155 us (0.68)
  waiting for transfers between devices: 152 us -> 82 us
  matrix products: 8.15 us -> 11.3 us
  starting transfers between devices: 16.2 us -> 13.2 us
  local copies, waits for them, and re-layouts: 12 us -> 9.4 us
    ppermute x8, waiting for transfers between devices: 72.5 us -> 0.02 us  [passed_along(): lax.ppermute(array, axis, [(i, (i + by) % count) for i in range(count)])]
    convert_element_type x10 -> x1, other arithmetic: 3.66 us -> 0.01 us  [on_device(): live = pair_live[0].astype(jnp.float32)]
    dot_general x12, matrix products: 8.15 us -> 11.3 us  [the longest x6 6.42 us: left_apply(): lax.dot_general(matrix, vector, (((1,), (0,)), ((), ())), precision=lax.P...]
    ppermute x8, starting transfers between devices: 16.1 us -> 13.1 us  [passed_along(): lax.ppermute(array, axis, [(i, (i + by) % count) for i in range(count)])]
    unnamed x4, waiting for transfers between devices: 79.4 us -> 81.9 us
    mul x0 -> x4, other arithmetic: none -> 2.42 us  [apply_dual(): back = live[slot] * right_apply(projected, coupling)]
    add x2 -> x4, other arithmetic: 0.02 us -> 2.43 us  [the longest x2 2.42 us: apply_dual(): inner = inner + live[slot] * left_apply(coupling, ahead)]
  transfers between devices with their start and end apart: 10 -> 10, of which waited for: 4 -> 2; matrix products, arithmetic and copies ran while one was open for 4% -> 11% of each run, Pallas kernels for 0% -> 0%
where the time goes in v1:
time: 155 us; the launch traced here: 154 us
  waiting for transfers between devices  82 us (53%)
  blocking collectives  19.3 us (12%)
  between operations  14.5 us (9%)
  starting transfers between devices  13.2 us (9%)
  matrix products  11.3 us (7%)
  local copies, waits for them, and re-layouts  9.4 us (6%)
  other arithmetic  4.85 us (3%)
    unnamed x4, waiting for transfers between devices  81.9 us
    all_gather x2, blocking collectives, on_device(): column = lax.all_gather(piece, 'row', axis=1, tiled=True)[0]  19.3 us
    ppermute x8, starting transfers between devices, passed_along(): lax.ppermute(array, axis, [(i, (i + by) % count) for i in range(count)])  13.1 us
    unnamed x10, local copies, waits for them, and re-layouts  6.72 us
    dot_general x6, matrix products, left_apply(): lax.dot_general(matrix, vector, (((1,), (0,)), ((), ())), precision=lax.P...  6.42 us
    dot_general x6, matrix products, right_apply(): jnp.dot(vector, matrix, precision=lax.Precision.HIGHEST, preferred_elemen...  4.84 us
  transfers between devices with their start and end apart: 10, of which 2 were waited for; matrix products, arithmetic and copies ran while one was open for 11% of the time, Pallas kernels for 0%

profile of v1, /device:TPU:0, one launch (start us, length us, event | category | flops | bytes accessed | tf_op | source)
XLA Modules:
  0.0 154.4 jit_solution(13610832899957684372)
XLA Ops:
  7.3 10.5 %all_gather.6 = f32[1,4096]{1,0:T(1,128)S(1)} all-gather(f32[1,512]{1,0:T(1,128)} %param.9), channel_id=1, replica_groups=mesh['row'=8,'col'=4] {'row'}, dimensions={1}, use_global_device_ids=true | all-gather | bytes 18432 | tf_op jit(solution)/shard_map/all_gather | solution.py:45
  17.9 3.7 %collective-permute-start.2 = (f32[768]{0:T(1024)S(1)}, f32[768]{0:T(1024)S(1)}, u32[]{:S(2)}, u32[]{:S(2)}) collective-permute-start(f32[768]{0:T(1024)S(1)} %dynamic-slice_reduce_fusion.1), channel_id=1, source_target_pairs={{0,3},{1,0},{2,1},{3,2},{4,7},{5,4},{6,5},{7,6},{8,11},{9,8},{10,9... | collective-permute-start | bytes 9224 | tf_op jit(solution)/shard_map/ppermute | solution.py:9
  21.5 1.1 fusion.73
  23.2 1.9 %fusion.30 = f32[768]{0:T(1024)S(1)} fusion(bf16[1,2,768,768]{3,2,1,0:T(8,128)(2,1)} %param.6, f32[1,768]{1,0:T(1,128)S(1)} %get-tuple-element.8), kind=kOutput, calls=%fused_computation.26 | convolution fusion | flops 7077888 | bytes 1185792 | tf_op jit(solution)/shard_map/dot_general | solution.py:20
  25.8 1.1 collective-permute-start
  28.0 2.0 %collective-permute-start.1 = (f32[768]{0:T(1024)S(1)}, f32[768]{0:T(1024)S(1)}, u32[]{:S(2)}, u32[]{:S(2)}) collective-permute-start(f32[768]{0:T(1024)S(1)} %broadcast_multiply_fusion.1), channel_id=1, source_target_pairs={{0,2},{1,3},{2,0},{3,1},{4,6},{5,7},{6,4},{7,5},{8,10},{9,11},{10,... | collective-permute-start | bytes 9224 | tf_op jit(solution)/shard_map/ppermute | solution.py:9
  30.0 1.1 fusion.33
  31.1 1.1 fusion.45
  32.2 1.2 multiply_add_fusion.1
  34.6 1.0 dynamic_update_slice.8
  35.6 2.0 %copy.6 = f32[1,4096]{0,1:T(8,128)} copy(f32[1,4096]{1,0:T(1,128)S(1)} %dynamic_update_slice.8) | data formatting | bytes 32768
  37.7 40.9 %reduce-scatter.7.cloned.1.call-done = f32[512,1]{1,0:T(8,128)} async-done(((f32[4096,1]{1,0:T(8,128)}), f32[512,1]{1,0:T(8,128)}) %reduce-scatter.7.cloned.1.call-update) | async-done | bytes 2064
  78.6 1.1 copy.7
  79.7 8.8 %all_gather.7 = f32[1,4096]{1,0:T(1,128)S(1)} all-gather(f32[1,512]{1,0:T(1,128)S(1)} %copy.7), channel_id=1, replica_groups=mesh['row'=8,'col'=4] {'row'}, dimensions={1}, use_global_device_ids=true | all-gather | bytes 18432 | tf_op jit(solution)/shard_map/all_gather | solution.py:45
  88.6 3.4 %collective-permute-start.6 = (f32[768]{0:T(1024)S(1)}, f32[768]{0:T(1024)S(1)}, u32[]{:S(2)}, u32[]{:S(2)}) collective-permute-start(f32[768]{0:T(1024)S(1)} %dynamic-slice_reduce_fusion), channel_id=1, source_target_pairs={{0,3},{1,0},{2,1},{3,2},{4,7},{5,4},{6,5},{7,6},{8,11},{9,8},{10,9... | collective-permute-start | bytes 9224 | tf_op jit(solution)/shard_map/ppermute | solution.py:9
  91.9 1.1 fusion.74
  94.9 1.2 collective-permute-start.4
  96.6 1.9 %collective-permute-start.5 = (f32[768]{0:T(1024)S(1)}, f32[768]{0:T(1024)S(1)}, u32[]{:S(2)}, u32[]{:S(2)}) collective-permute-start(f32[768]{0:T(1024)S(1)} %broadcast_multiply_fusion), channel_id=1, source_target_pairs={{0,2},{1,3},{2,0},{3,1},{4,6},{5,7},{6,4},{7,5},{8,10},{9,11},{10,... | collective-permute-start | bytes 9224 | tf_op jit(solution)/shard_map/ppermute | solution.py:9
  98.5 1.1 fusion.39
  99.6 1.1 fusion.51
  100.7 1.2 multiply_add_fusion
  102.9 2.0 %copy.8 = f32[1,4096]{0,1:T(8,128)} copy(f32[1,4096]{1,0:T(1,128)S(1)} %dynamic_update_slice.9) | data formatting | bytes 32768
  104.9 41.0 %reduce-scatter.9.cloned.1.call-done = f32[512,1]{1,0:T(8,128)} async-done(((f32[4096,1]{1,0:T(8,128)}), f32[512,1]{1,0:T(8,128)}) %reduce-scatter.9.cloned.1.call-update) | async-done | bytes 2064
  145.9 1.6 %copy.9 = f32[1,512]{1,0:T(1,128)} copy(f32[1,512]{0,1:T(8,128)} %bitcast.90) | data formatting | bytes 4096
  (46 shorter events, 7.2 us)
Async XLA Ops:
  6.5 15.0 %copy-start = (bf16[1,768,768]{2,1,0:T(8,128)(2,1)S(1)}, bf16[1,768,768]{2,1,0:T(8,128)(2,1)}, u32[]{:S(2)}) copy-start(bf16[1,768,768]{2,1,0:T(8,128)(2,1)} %param.5) | copy-start | bytes 3538948
  6.5 72.1 %reduce-scatter.7.cloned.1.call-start = ((), (), s32[]{:S(2)}) async-start(), calls=%async_computation.2 | async-start | bytes 2359296
  17.8 4.9 %copy-start.2 = (s32[1,2]{1,0:T(1,128)S(1)}, s32[1,2]{1,0:T(1,128)}, u32[]{:S(2)}) copy-start(s32[1,2]{1,0:T(1,128)} %param.7) | copy-start | bytes 28
  17.9 8.9 %copy-start.1 = (bf16[1,2,768,768]{3,2,1,0:T(8,128)(2,1)S(1)}, bf16[1,2,768,768]{3,2,1,0:T(8,128)(2,1)}, u32[]{:S(2)}) copy-start(bf16[1,2,768,768]{3,2,1,0:T(8,128)(2,1)} %param.6) | copy-start | bytes 7077892
  17.9 12.1 %collective-permute-start.2 = (f32[768]{0:T(1024)S(1)}, f32[768]{0:T(1024)S(1)}, u32[]{:S(2)}, u32[]{:S(2)}) collective-permute-start(f32[768]{0:T(1024)S(1)} %dynamic-slice_reduce_fusion.1), channel_id=1, source_target_pairs={{0,3},{1,0},{2,1},{3,2},{4,7},{5,4},{6,5},{7,6},{8,11},{9,8},{10,9... | collective-permute-start | bytes 9224 | tf_op jit(solution)/shard_map/ppermute | solution.py:9
  21.5 9.5 %collective-permute-start.3 = (f32[768]{0:T(1024)S(1)}, f32[768]{0:T(1024)S(1)}, u32[]{:S(2)}, u32[]{:S(2)}) collective-permute-start(f32[768]{0:T(1024)S(1)} %dynamic-slice_reduce_fusion.1), channel_id=1, source_target_pairs={{0,2},{1,3},{2,0},{3,1},{4,6},{5,7},{6,4},{7,5},{8,10},{9,11},{10,... | collective-permute-start | bytes 9224 | tf_op jit(solution)/shard_map/ppermute | solution.py:9
  25.8 8.2 %collective-permute-start = (f32[768]{0:T(1024)S(1)}, f32[768]{0:T(1024)S(1)}, u32[]{:S(2)}, u32[]{:S(2)}) collective-permute-start(f32[768]{0:T(1024)S(1)} %broadcast_multiply_fusion.3), channel_id=1, source_target_pairs={{0,1},{1,2},{2,3},{3,0},{4,5},{5,6},{6,7},{7,4},{8,9},{9,10},{10,1... | collective-permute-start | bytes 9224 | tf_op jit(solution)/shard_map/ppermute | solution.py:9
  28.0 6.0 %collective-permute-start.1 = (f32[768]{0:T(1024)S(1)}, f32[768]{0:T(1024)S(1)}, u32[]{:S(2)}, u32[]{:S(2)}) collective-permute-start(f32[768]{0:T(1024)S(1)} %broadcast_multiply_fusion.1), channel_id=1, source_target_pairs={{0,2},{1,3},{2,0},{3,1},{4,6},{5,7},{6,4},{7,5},{8,10},{9,11},{10,... | collective-permute-start | bytes 9224 | tf_op jit(solution)/shard_map/ppermute | solution.py:9
  37.6 108.3 %reduce-scatter.9.cloned.1.call-start = ((), (), s32[]{:S(2)}) async-start(), calls=%async_computation.3 | async-start | bytes 2359296
  88.6 10.0 %collective-permute-start.6 = (f32[768]{0:T(1024)S(1)}, f32[768]{0:T(1024)S(1)}, u32[]{:S(2)}, u32[]{:S(2)}) collective-permute-start(f32[768]{0:T(1024)S(1)} %dynamic-slice_reduce_fusion), channel_id=1, source_target_pairs={{0,3},{1,0},{2,1},{3,2},{4,7},{5,4},{6,5},{7,6},{8,11},{9,8},{10,9... | collective-permute-start | bytes 9224 | tf_op jit(solution)/shard_map/ppermute | solution.py:9
  91.9 7.7 %collective-permute-start.7 = (f32[768]{0:T(1024)S(1)}, f32[768]{0:T(1024)S(1)}, u32[]{:S(2)}, u32[]{:S(2)}) collective-permute-start(f32[768]{0:T(1024)S(1)} %dynamic-slice_reduce_fusion), channel_id=1, source_target_pairs={{0,2},{1,3},{2,0},{3,1},{4,6},{5,7},{6,4},{7,5},{8,10},{9,11},{10,... | collective-permute-start | bytes 9224 | tf_op jit(solution)/shard_map/ppermute | solution.py:9
  94.9 7.6 %collective-permute-start.4 = (f32[768]{0:T(1024)S(1)}, f32[768]{0:T(1024)S(1)}, u32[]{:S(2)}, u32[]{:S(2)}) collective-permute-start(f32[768]{0:T(1024)S(1)} %broadcast_multiply_fusion.2), channel_id=1, source_target_pairs={{0,1},{1,2},{2,3},{3,0},{4,5},{5,6},{6,7},{7,4},{8,9},{9,10},{10,1... | collective-permute-start | bytes 9224 | tf_op jit(solution)/shard_map/ppermute | solution.py:9
  96.6 5.9 %collective-permute-start.5 = (f32[768]{0:T(1024)S(1)}, f32[768]{0:T(1024)S(1)}, u32[]{:S(2)}, u32[]{:S(2)}) collective-permute-start(f32[768]{0:T(1024)S(1)} %broadcast_multiply_fusion), channel_id=1, source_target_pairs={{0,2},{1,3},{2,0},{3,1},{4,6},{5,7},{6,4},{7,5},{8,10},{9,11},{10,... | collective-permute-start | bytes 9224 | tf_op jit(solution)/shard_map/ppermute | solution.py:9
Sparse Core Ops, SparseCore 0:
  37.8 40.8 reduce-scatter.6
  105.1 40.8 reduce-scatter.8

commit v2 on v1

v2 whole, which is shorter than its diff:
```python
import jax
import jax.numpy as jnp
from jax import lax
from jax.experimental import pallas as pl
from jax.experimental.pallas import tpu as pltpu
from jax.sharding import PartitionSpec as P

LANES = 128
MESH = pl.DeviceIdType.MESH


def split_rows(vector):
    high = vector.astype(jnp.bfloat16).astype(jnp.float32)
    rest = vector - high
    middle = rest.astype(jnp.bfloat16).astype(jnp.float32)
    lowest = rest - middle
    row = lax.broadcasted_iota(jnp.int32, vector.shape, 0)
    picked = jnp.where(row == 0, high, jnp.where(row == 1, middle, lowest))
    return jnp.where(row < 3, picked, 0.0).astype(jnp.bfloat16)


def spread(products):
    return jnp.broadcast_to(jnp.sum(products, axis=0, keepdims=True), products.shape)


def left_apply(matrix, vector):
    return spread(lax.dot_general(
        split_rows(vector), matrix, (((1,), (1,)), ((), ())),
        preferred_element_type=jnp.float32,
    ))


def right_apply(rows, matrix):
    return spread(jnp.dot(rows, matrix, preferred_element_type=jnp.float32))


def kernel(n_row, n_col, hops, basis_hbm, coupling_hbm, live_ref, offset_ref, dual_ref, out_ref,
           mats, gathered, column, placing, outgoing, incoming, sums, far_offsets,
           load_sems, send_sems, recv_sems, offset_send, offset_recv):
    me_row, me_col = lax.axis_index("row"), lax.axis_index("col")
    sides = hops + 1
    part_rows = dual_ref.shape[0]
    rows = n_row * part_rows
    width = mats.shape[2]
    chunks = width // LANES
    others = sides * n_row - 1

    loads = [pltpu.make_async_copy(basis_hbm.at[0], mats.at[0], load_sems.at[0])]
    for h in range(hops):
        loads.append(pltpu.make_async_copy(coupling_hbm.at[0, h], mats.at[h + 1], load_sems.at[h + 1]))
    for load in loads:
        load.start()

    barrier = pltpu.get_barrier_semaphore()
    shifts = sorted({d % n_col for d in range(-hops, hops + 1)})
    for shift in shifts:
        col = lax.rem(me_col + shift, n_col)

        def greet(i, carry, col=col):
            pl.semaphore_signal(barrier, inc=1, device_id=(lax.rem(me_row + i, n_row), col), device_id_type=MESH)
            return carry

        lax.fori_loop(1 if shift == 0 else 0, n_row, greet, 0, unroll=True)

    for k in range(sides):
        column[k, rows:, :] = jnp.zeros((column.shape[1] - rows, LANES), jnp.float32)
        placing[k, :, :] = jnp.zeros(placing.shape[1:], jnp.float32)
    pl.semaphore_wait(barrier, len(shifts) * n_row - 1)

    offset_copies = []
    for h in range(hops):
        copy = pltpu.make_async_remote_copy(
            src_ref=offset_ref, dst_ref=far_offsets.at[h],
            send_sem=offset_send.at[h], recv_sem=offset_recv.at[h],
            device_id=(me_row, lax.rem(me_col + n_col - (h + 1), n_col)), device_id_type=MESH)
        copy.start()
        offset_copies.append(copy)

    lane = lax.broadcasted_iota(jnp.int32, (8, LANES), 1)
    sub = lax.broadcasted_iota(jnp.int32, (8, LANES), 0)

    def gather_start(app, source):
        for k in range(sides):
            col = lax.rem(me_col + n_col - k, n_col)

            def send(i, carry, k=k, col=col):
                pltpu.make_async_remote_copy(
                    src_ref=source, dst_ref=gathered.at[app, k * n_row + me_row],
                    send_sem=send_sems.at[2 * app], recv_sem=recv_sems.at[2 * app],
                    device_id=(lax.rem(me_row + i, n_row), col), device_id_type=MESH).start()
                return carry

            lax.fori_loop(1 if k == 0 else 0, n_row, send, 0, unroll=True)
        gathered[app, me_row] = source[...]

    def wait_all(ref, sem):
        pltpu.make_async_copy(ref.at[pl.ds(0, others)], ref.at[pl.ds(0, others)], sem).wait()

    def window(k, start):
        first = start // LANES
        within = start - first * LANES
        tile = column[k, pl.ds(first, 8), :]
        turned = pltpu.roll(tile, lax.rem(LANES - within, LANES), 1)
        after = pltpu.roll(turned, 7, 0)
        cut = jnp.where(lane < LANES - within, turned, after)
        return jnp.concatenate(
            [jnp.broadcast_to(cut[j:j + 1, :], (8, LANES)) for j in range(chunks)], axis=1)

    def place(k, start, vector):
        first = start // LANES
        within = start - first * LANES
        tile = jnp.zeros((8, LANES), jnp.float32)
        for j in range(chunks):
            tile = jnp.where(sub == j, vector[:, j * LANES:(j + 1) * LANES], tile)
        turned = pltpu.roll(tile, within, 1)
        before = pltpu.roll(turned, 1, 0)
        placing[k, rows:rows + 8, :] = jnp.where(lane >= within, turned, before)
        return first

    starts = None
    lives = [live_ref[0, h].astype(jnp.float32) for h in range(hops)]
    source = dual_ref
    for app in range(2):
        gather_start(app, source)
        if app == 0:
            for copy in offset_copies:
                copy.wait()
            starts = [offset_ref[0]] + [far_offsets[h, 0] for h in range(hops)]
        wait_all(gathered.at[app], recv_sems.at[2 * app])
        for k in range(sides):
            for r in range(n_row):
                column[k, r * part_rows:(r + 1) * part_rows, :] = gathered[app, k * n_row + r]
        windows = [window(k, starts[k]) for k in range(sides)]
        if app == 0:
            for load in loads:
                load.wait()
        projected = left_apply(mats[0], windows[0])
        inner = projected
        for h in range(hops):
            inner = inner + lives[h] * left_apply(mats[h + 1], windows[h + 1])
        seen = split_rows(projected)
        totals = [lives[h] * right_apply(seen, mats[h + 1]) for h in range(hops)]
        totals = [right_apply(split_rows(inner), mats[0])] + totals
        for k in range(sides):
            first = place(k, starts[k], totals[k])
            col = lax.rem(me_col + k, n_col)
            for t in range(n_row):
                outgoing[app, k * n_row + t] = placing[k, pl.ds(rows - first + t * part_rows, part_rows), :]

            def send(i, carry, k=k, col=col):
                row = lax.rem(me_row + i, n_row)
                pltpu.make_async_remote_copy(
                    src_ref=outgoing.at[app, k * n_row + row], dst_ref=incoming.at[app, k * n_row + me_row],
                    send_sem=send_sems.at[2 * app + 1], recv_sem=recv_sems.at[2 * app + 1],
                    device_id=(row, col), device_id_type=MESH).start()
                return carry

            lax.fori_loop(1 if k == 0 else 0, n_row, send, 0, unroll=True)
        incoming[app, me_row] = outgoing[app, me_row]
        wait_all(incoming.at[app], recv_sems.at[2 * app + 1])
        summed = jnp.sum(incoming[app], axis=0)
        if app == 0:
            sums[...] = summed
            source = sums
        else:
            out_ref[...] = summed
    for app in range(2):
        wait_all(gathered.at[app], send_sems.at[2 * app])
        wait_all(outgoing.at[app], send_sems.at[2 * app + 1])


def on_device(sub_basis, coupling, pair_live, offsets, dual_in):
    n_row, n_col = lax.axis_size("row"), lax.axis_size("col")
    hops = coupling.shape[1]
    sides = hops + 1
    size = dual_in.shape[1]
    part_rows = size // LANES
    rows = n_row * part_rows
    depth, width = sub_basis.shape[1:]
    smem = pl.BlockSpec(memory_space=pltpu.SMEM)
    vmem = pl.BlockSpec(memory_space=pltpu.VMEM)
    hbm = pl.BlockSpec(memory_space=pl.ANY)
    out = pl.pallas_call(
        lambda *refs: kernel(n_row, n_col, hops, *refs),
        out_shape=jax.ShapeDtypeStruct((part_rows, LANES), jnp.float32),
        in_specs=[hbm, hbm, smem, smem, vmem],
        out_specs=vmem,
        scratch_shapes=[
            pltpu.VMEM((sides, depth, width), jnp.bfloat16),
            pltpu.VMEM((2, sides * n_row, part_rows, LANES), jnp.float32),
            pltpu.VMEM((sides, rows + 8, LANES), jnp.float32),
            pltpu.VMEM((sides, 2 * rows + 8, LANES), jnp.float32),
            pltpu.VMEM((2, sides * n_row, part_rows, LANES), jnp.float32),
            pltpu.VMEM((2, sides * n_row, part_rows, LANES), jnp.float32),
            pltpu.VMEM((part_rows, LANES), jnp.float32),
            pltpu.SMEM((hops, 1), jnp.int32),
            pltpu.SemaphoreType.DMA((sides,)),
            pltpu.SemaphoreType.DMA((4,)),
            pltpu.SemaphoreType.DMA((4,)),
            pltpu.SemaphoreType.DMA((hops,)),
            pltpu.SemaphoreType.DMA((hops,)),
        ],
        compiler_params=pltpu.CompilerParams(
            collective_id=0, has_side_effects=True, vmem_limit_bytes=32 * 1024 * 1024),
    )(sub_basis, coupling, pair_live, offsets, dual_in.reshape(part_rows, LANES))
    return out.reshape(1, size)


def solution(mesh):
    return jax.shard_map(
        on_device,
        mesh=mesh,
        in_specs=(
            P(("row", "col"), None, None),
            P(("row", "col"), None, None, None),
            P(("row", "col"), None),
            P(("row", "col")),
            P("col", "row"),
        ),
        out_specs=P("col", "row"),
        check_vma=False,
    )
```

time: 155 us -> 35.5 us (0.23)
  waiting for transfers between devices: 82 us -> 0 us
  Pallas kernels: 0 us -> 29.8 us
  blocking collectives: 19.3 us -> 0 us
  between operations: 14.5 us -> 0.67 us
  starting transfers between devices: 13.2 us -> 0 us
  matrix products: 11.3 us -> 0 us
  other arithmetic: 4.85 us -> 0 us
  local copies, waits for them, and re-layouts: 9.4 us -> 4.84 us
    unnamed x4 -> x0, waiting for transfers between devices: 81.9 us -> none
    pallas_call x0 -> x1, Pallas kernels: none -> 29.8 us  [on_device(): pl.pallas_call(lambda *refs: kernel(n_row, n_col, hops, *refs), out_shape...]
    all_gather x2 -> x0, blocking collectives: 19.3 us -> none  [on_device(): column = lax.all_gather(piece, 'row', axis=1, tiled=True)[0]]
    ppermute x8 -> x0, starting transfers between devices: 13.1 us -> none  [passed_along(): lax.ppermute(array, axis, [(i, (i + by) % count) for i in range(count)])]
    dot_general x12 -> x0, matrix products: 11.3 us -> none  [the longest x6 6.42 us: left_apply(): lax.dot_general(matrix, vector, (((1,), (0,)), ((), ())), precision=lax.P...]
    add x4 -> x0, other arithmetic: 2.43 us -> none  [the longest x2 2.42 us: apply_dual(): inner = inner + live[slot] * left_apply(coupling, ahead)]
    mul x4 -> x0, other arithmetic: 2.42 us -> none  [apply_dual(): back = live[slot] * right_apply(projected, coupling)]
    unnamed x10 -> x9, local copies, waits for them, and re-layouts: 6.72 us -> 4.84 us
  transfers between devices with their start and end apart: 10 -> 0, of which waited for: 2 -> 0; matrix products, arithmetic and copies ran while one was open for 11% -> 0% of each run, Pallas kernels for 0% -> 0%
where the time goes in v2:
time: 35.5 us; the launch traced here: 35.3 us
  Pallas kernels  29.8 us (84%)
  local copies, waits for them, and re-layouts  4.84 us (14%)
  between operations  0.67 us (2%)
    pallas_call x1, Pallas kernels, on_device(): pl.pallas_call(lambda *refs: kernel(n_row, n_col, hops, *refs), out_shape...  29.8 us
    unnamed x9, local copies, waits for them, and re-layouts  4.84 us

profile of v2, /device:TPU:0, one launch (start us, length us, event | category | flops | bytes accessed | tf_op | source)
XLA Modules:
  0.0 35.3 jit_solution(1149720367677631582)
XLA Ops:
  0.7 0.0 copy-start
  0.7 1.7 %copy-done = bf16[1,2,768,768]{3,2,1,0:T(8,128)(2,1)S(1)} copy-done((bf16[1,2,768,768]{3,2,1,0:T(8,128)(2,1)S(1)}, bf16[1,2,768,768]{3,2,1,0:T(8,128)(2,1)}, u32[]{:S(2)}) %copy-start) | copy-done | bytes 2359320
  2.3 0.0 copy-start.1
  2.3 1.3 %copy-done.1 = bf16[1,768,768]{2,1,0:T(8,128)(2,1)S(1)} copy-done((bf16[1,768,768]{2,1,0:T(8,128)(2,1)S(1)}, bf16[1,768,768]{2,1,0:T(8,128)(2,1)}, u32[]{:S(2)}) %copy-start.1) | copy-done | bytes 1179672
  3.6 0.0 copy-start.2
  3.6 0.7 %copy-done.2 = f32[1,512]{1,0:T(1,128)S(1)} copy-done((f32[1,512]{1,0:T(1,128)S(1)}, f32[1,512]{1,0:T(1,128)}, u32[]{:S(2)}) %copy-start.2) | copy-done | bytes 2072
  4.3 0.0 copy-start.3
  4.3 0.7 %copy-done.3 = s32[1,2]{1,0:T(1,128)S(1)} copy-done((s32[1,2]{1,0:T(1,128)S(1)}, s32[1,2]{1,0:T(1,128)}, u32[]{:S(2)}) %copy-start.3) | copy-done | bytes 32
  4.9 29.8 %shard_map.55 = f32[4,128]{1,0:T(4,128)S(1)} custom-call(bf16[1,768,768]{2,1,0:T(8,128)(2,1)S(1)} %copy-done.1, bf16[1,2,768,768]{3,2,1,0:T(8,128)(2,1)S(1)} %copy-done, s32[1,2]{1,0:T(1,128)S(1)} %copy-done.3, s32[1]{0:T(128)S(6)} %copy.7.refs_3_, f32[4,128]{1,0:T(4,128)S(1)} %bitcast.3), custom_call_target="tpu_custom_call" | custom-call | tf_op jit(solution)/shard_map/pallas_call | solution.py:183
  34.7 0.6 %copy.8 = f32[1,512]{1,0:T(1,128)} copy(f32[1,512]{1,0:T(1,128)S(1)} %bitcast.2) | data formatting | bytes 4096
Async XLA Ops:
  0.7 1.7 %copy-start = (bf16[1,2,768,768]{3,2,1,0:T(8,128)(2,1)S(1)}, bf16[1,2,768,768]{3,2,1,0:T(8,128)(2,1)}, u32[]{:S(2)}) copy-start(bf16[1,2,768,768]{3,2,1,0:T(8,128)(2,1)} %refs_1_.1) | copy-start | bytes 7077892
  2.3 1.3 %copy-start.1 = (bf16[1,768,768]{2,1,0:T(8,128)(2,1)S(1)}, bf16[1,768,768]{2,1,0:T(8,128)(2,1)}, u32[]{:S(2)}) copy-start(bf16[1,768,768]{2,1,0:T(8,128)(2,1)} %refs_0_.1) | copy-start | bytes 3538948
  3.6 0.7 %copy-start.2 = (f32[1,512]{1,0:T(1,128)S(1)}, f32[1,512]{1,0:T(1,128)}, u32[]{:S(2)}) copy-start(f32[1,512]{1,0:T(1,128)} %param.9) | copy-start | bytes 6148
  4.3 0.7 %copy-start.3 = (s32[1,2]{1,0:T(1,128)S(1)}, s32[1,2]{1,0:T(1,128)}, u32[]{:S(2)}) copy-start(s32[1,2]{1,0:T(1,128)} %refs_2_.1) | copy-start | bytes 28

commit v3 on v1

v3 whole, which is shorter than its diff:
```python
import jax
import jax.numpy as jnp
from jax import lax
from jax.experimental import pallas as pl
from jax.experimental.pallas import tpu as pltpu
from jax.sharding import PartitionSpec as P

LANES = 128
MESH = pl.DeviceIdType.MESH


def split_rows(vector):
    high = vector.astype(jnp.bfloat16).astype(jnp.float32)
    rest = vector - high
    middle = rest.astype(jnp.bfloat16).astype(jnp.float32)
    lowest = rest - middle
    row = lax.broadcasted_iota(jnp.int32, vector.shape, 0)
    picked = jnp.where(row == 0, high, jnp.where(row == 1, middle, lowest))
    return jnp.where(row < 3, picked, 0.0).astype(jnp.bfloat16)


def spread(products):
    return jnp.broadcast_to(jnp.sum(products, axis=0, keepdims=True), products.shape)


def left_apply(matrix, vector):
    return spread(lax.dot_general(
        split_rows(vector), matrix, (((1,), (1,)), ((), ())),
        preferred_element_type=jnp.float32,
    ))


def right_apply(rows, matrix):
    return spread(jnp.dot(rows, matrix, preferred_element_type=jnp.float32))


def to_lanes(tile, chunks):
    return jnp.concatenate(
        [jnp.broadcast_to(tile[j:j + 1, :], (8, LANES)) for j in range(chunks)], axis=1)


def to_tile(vector, chunks):
    row = lax.broadcasted_iota(jnp.int32, (8, LANES), 0)
    tile = jnp.zeros((8, LANES), jnp.float32)
    for j in range(chunks):
        tile = jnp.where(row == j, vector[:, j * LANES:(j + 1) * LANES], tile)
    return tile


def kernel(n_row, n_col, hops, basis_hbm, coupling_hbm, live_hbm, offset_hbm, dual_hbm, out_ref,
           mats, gathered, column, cut_window, far_window, back_out, back_in, placing, outgoing, incoming,
           live_ref, offset_ref, load_sems, small_sems, gather_send, gather_recv,
           window_send, window_recv, back_send, back_recv, scatter_send, scatter_recv):
    me_row, me_col = lax.axis_index("row"), lax.axis_index("col")
    part_rows = dual_hbm.shape[0]
    rows = n_row * part_rows
    chunks = mats.shape[2] // LANES
    others = n_row - 1

    small = [
        pltpu.make_async_copy(dual_hbm, gathered.at[0, me_row], small_sems.at[0]),
        pltpu.make_async_copy(offset_hbm, offset_ref, small_sems.at[1]),
        pltpu.make_async_copy(live_hbm, live_ref, small_sems.at[2]),
    ]
    loads = [pltpu.make_async_copy(basis_hbm.at[0], mats.at[0], load_sems.at[0])]
    for h in range(hops):
        loads.append(pltpu.make_async_copy(coupling_hbm.at[0, h], mats.at[h + 1], load_sems.at[h + 1]))
    for copy in small + loads:
        copy.start()

    barrier = pltpu.get_barrier_semaphore()
    for i in range(1, n_row):
        pl.semaphore_signal(barrier, inc=1, device_id=(lax.rem(me_row + i, n_row), me_col), device_id_type=MESH)
    shifts = sorted({d % n_col for d in range(-hops, hops + 1)} - {0})
    for shift in shifts:
        pl.semaphore_signal(barrier, inc=1, device_id=(me_row, lax.rem(me_col + shift, n_col)), device_id_type=MESH)

    column[rows:, :] = jnp.zeros((column.shape[0] - rows, LANES), jnp.float32)
    placing[...] = jnp.zeros(placing.shape, jnp.float32)
    for copy in small:
        copy.wait()
    start = offset_ref[0]
    first = start // LANES
    within = start - first * LANES
    lives = [live_ref[0, h].astype(jnp.float32) for h in range(hops)]
    lane = lax.broadcasted_iota(jnp.int32, (8, LANES), 1)
    pl.semaphore_wait(barrier, others + len(shifts))

    def row_peer(i):
        return lax.rem(me_row + i, n_row)

    def col_peer(shift):
        return (me_row, lax.rem(me_col + (shift % n_col), n_col))

    def wait_others(ref, sem):
        pltpu.make_async_copy(ref.at[pl.ds(0, others)], ref.at[pl.ds(0, others)], sem).wait()

    pending = []
    for app in range(2):
        for i in range(1, n_row):
            pltpu.make_async_remote_copy(
                src_ref=gathered.at[app, me_row], dst_ref=gathered.at[app, me_row],
                send_sem=gather_send.at[app], recv_sem=gather_recv.at[app],
                device_id=(row_peer(i), me_col), device_id_type=MESH).start()
        wait_others(gathered.at[app], gather_recv.at[app])
        for r in range(n_row):
            column[r * part_rows:(r + 1) * part_rows, :] = gathered[app, r]
        tile = column[pl.ds(first, 8), :]
        turned = pltpu.roll(tile, lax.rem(LANES - within, LANES), 1)
        cut = jnp.where(lane < LANES - within, turned, pltpu.roll(turned, 7, 0))
        cut_window[app] = cut
        windows, backs = [], []
        for h in range(hops):
            slot = app * hops + h
            copy = pltpu.make_async_remote_copy(
                src_ref=cut_window.at[app], dst_ref=far_window.at[slot],
                send_sem=window_send.at[slot], recv_sem=window_recv.at[slot],
                device_id=col_peer(-(h + 1)), device_id_type=MESH)
            copy.start()
            windows.append(copy)
        if app == 0:
            for load in loads:
                load.wait()
        projected = left_apply(mats[0], to_lanes(cut, chunks))
        seen = split_rows(projected)
        for h in range(hops):
            slot = app * hops + h
            back_out[slot] = lives[h] * to_tile(right_apply(seen, mats[h + 1]), chunks)
            copy = pltpu.make_async_remote_copy(
                src_ref=back_out.at[slot], dst_ref=back_in.at[slot],
                send_sem=back_send.at[slot], recv_sem=back_recv.at[slot],
                device_id=col_peer(h + 1), device_id_type=MESH)
            copy.start()
            backs.append(copy)
        inner = projected
        for h in range(hops):
            windows[h].wait_recv()
            inner = inner + lives[h] * left_apply(mats[h + 1], to_lanes(far_window[app * hops + h], chunks))
        total = to_tile(right_apply(split_rows(inner), mats[0]), chunks)
        for h in range(hops):
            backs[h].wait_recv()
            total = total + back_in[app * hops + h]
        turned = pltpu.roll(total, within, 1)
        placing[rows:rows + 8, :] = jnp.where(lane >= within, turned, pltpu.roll(turned, 1, 0))
        for t in range(n_row):
            outgoing[app, t] = placing[pl.ds(rows - first + t * part_rows, part_rows), :]
        for i in range(1, n_row):
            pltpu.make_async_remote_copy(
                src_ref=outgoing.at[app, row_peer(i)], dst_ref=incoming.at[app, me_row],
                send_sem=scatter_send.at[app], recv_sem=scatter_recv.at[app],
                device_id=(row_peer(i), me_col), device_id_type=MESH).start()
        incoming[app, me_row] = outgoing[app, me_row]
        wait_others(incoming.at[app], scatter_recv.at[app])
        summed = jnp.sum(incoming[app], axis=0)
        if app == 0:
            gathered[1, me_row] = summed
        else:
            out_ref[...] = summed
        pending += windows + backs
    for app in range(2):
        wait_others(gathered.at[app], gather_send.at[app])
        wait_others(outgoing.at[app], scatter_send.at[app])
    for copy in pending:
        copy.wait_send()


def on_device(sub_basis, coupling, pair_live, offsets, dual_in):
    n_row, n_col = lax.axis_size("row"), lax.axis_size("col")
    hops = coupling.shape[1]
    size = dual_in.shape[1]
    part_rows = size // LANES
    rows = n_row * part_rows
    depth, width = sub_basis.shape[1:]
    hbm = pl.BlockSpec(memory_space=pltpu.HBM)
    tiles = pltpu.VMEM((2 * hops, 8, LANES), jnp.float32)
    parts = pltpu.VMEM((2, n_row, part_rows, LANES), jnp.float32)
    dma = pltpu.SemaphoreType.DMA
    out = pl.pallas_call(
        lambda *refs: kernel(n_row, n_col, hops, *refs),
        out_shape=jax.ShapeDtypeStruct((part_rows, LANES), jnp.float32),
        in_specs=[hbm] * 5,
        out_specs=pl.BlockSpec(memory_space=pltpu.VMEM),
        scratch_shapes=[
            pltpu.VMEM((hops + 1, depth, width), jnp.bfloat16),
            parts,
            pltpu.VMEM((rows + 8, LANES), jnp.float32),
            pltpu.VMEM((2, 8, LANES), jnp.float32),
            tiles, tiles, tiles,
            pltpu.VMEM((2 * rows + 8, LANES), jnp.float32),
            parts, parts,
            pltpu.SMEM(pair_live.shape, jnp.int32),
            pltpu.SMEM(offsets.shape, jnp.int32),
            dma((hops + 1,)), dma((3,)), dma((2,)), dma((2,)),
            dma((2 * hops,)), dma((2 * hops,)), dma((2 * hops,)), dma((2 * hops,)),
            dma((2,)), dma((2,)),
        ],
        compiler_params=pltpu.CompilerParams(
            collective_id=0, has_side_effects=True, vmem_limit_bytes=60 * 1024 * 1024),
    )(sub_basis, coupling, pair_live, offsets, dual_in.reshape(part_rows, LANES))
    return out.reshape(1, size)


def solution(mesh):
    return jax.shard_map(
        on_device,
        mesh=mesh,
        in_specs=(
            P(("row", "col"), None, None),
            P(("row", "col"), None, None, None),
            P(("row", "col"), None),
            P(("row", "col")),
            P("col", "row"),
        ),
        out_specs=P("col", "row"),
        check_vma=False,
    )
```

time: 155 us -> 29.8 us (0.19)
  waiting for transfers between devices: 82 us -> 0 us
  Pallas kernels: 0 us -> 27.7 us
  blocking collectives: 19.3 us -> 0 us
  between operations: 14.5 us -> 0.66 us
  starting transfers between devices: 13.2 us -> 0 us
  matrix products: 11.3 us -> 0 us
  local copies, waits for them, and re-layouts: 9.4 us -> 1.26 us
  other arithmetic: 4.85 us -> 0 us
    unnamed x4 -> x0, waiting for transfers between devices: 81.9 us -> none
    pallas_call x0 -> x1, Pallas kernels: none -> 27.7 us  [on_device(): pl.pallas_call(lambda *refs: kernel(n_row, n_col, hops, *refs), out_shape...]
    all_gather x2 -> x0, blocking collectives: 19.3 us -> none  [on_device(): column = lax.all_gather(piece, 'row', axis=1, tiled=True)[0]]
    ppermute x8 -> x0, starting transfers between devices: 13.1 us -> none  [passed_along(): lax.ppermute(array, axis, [(i, (i + by) % count) for i in range(count)])]
    dot_general x12 -> x0, matrix products: 11.3 us -> none  [the longest x6 6.42 us: left_apply(): lax.dot_general(matrix, vector, (((1,), (0,)), ((), ())), precision=lax.P...]
    unnamed x10 -> x1, local copies, waits for them, and re-layouts: 6.72 us -> 1.26 us
    add x4 -> x0, other arithmetic: 2.43 us -> none  [the longest x2 2.42 us: apply_dual(): inner = inner + live[slot] * left_apply(coupling, ahead)]
    mul x4 -> x0, other arithmetic: 2.42 us -> none  [apply_dual(): back = live[slot] * right_apply(projected, coupling)]
  transfers between devices with their start and end apart: 10 -> 0, of which waited for: 2 -> 0; matrix products, arithmetic and copies ran while one was open for 11% -> 0% of each run, Pallas kernels for 0% -> 0%
where the time goes in v3:
time: 29.8 us; the launch traced here: 29.6 us
  Pallas kernels  27.7 us (93%)
  local copies, waits for them, and re-layouts  1.26 us (4%)
  between operations  0.66 us (2%)
    pallas_call x1, Pallas kernels, on_device(): pl.pallas_call(lambda *refs: kernel(n_row, n_col, hops, *refs), out_shape...  27.7 us
    unnamed x1, local copies, waits for them, and re-layouts  1.26 us

profile of v3, /device:TPU:0, one launch (start us, length us, event | category | flops | bytes accessed | tf_op | source)
XLA Modules:
  0.0 29.6 jit_solution(10093593315219538596)
XLA Ops:
  0.7 27.7 %shard_map.55 = f32[4,128]{1,0:T(4,128)} custom-call(bf16[1,768,768]{2,1,0:T(8,128)(2,1)} %refs_0_.1, bf16[1,2,768,768]{3,2,1,0:T(8,128)(2,1)} %refs_1_.1, s32[1,2]{1,0:T(1,128)} %refs_2_.1, s32[1]{0:T(128)S(6)} %copy.7.refs_3_, f32[4,128]{1,0:T(4,128)} %bitcast.3), custom_call_target="tpu_custom_call" | custom-call | tf_op jit(solution)/shard_map/pallas_call | solution.py:178
  28.4 1.3 %copy.8 = f32[1,512]{1,0:T(1,128)} copy(f32[1,512]{1,0:T(1,128)} %bitcast.2) | data formatting | bytes 4096

commit v4 on v3

--- a/solution.py
+++ b/solution.py
@@ -48,9 +48,9 @@
 
 
 def kernel(n_row, n_col, hops, basis_hbm, coupling_hbm, live_hbm, offset_hbm, dual_hbm, out_ref,
-           mats, gathered, column, cut_window, far_window, back_out, back_in, placing, outgoing, incoming,
+           mats, gathered, column, middle, row_offsets, cut_window, far_window, back_out, back_in, placing, outgoing, incoming,
            live_ref, offset_ref, load_sems, small_sems, gather_send, gather_recv,
-           window_send, window_recv, back_send, back_recv, scatter_send, scatter_recv):
+           middle_send, middle_recv, offset_send, offset_recv, window_send, window_recv, back_send, back_recv, scatter_send, scatter_recv):
     me_row, me_col = lax.axis_index("row"), lax.axis_index("col")
     part_rows = dual_hbm.shape[0]
     rows = n_row * part_rows
@@ -58,7 +58,7 @@
     others = n_row - 1
 
     small = [
-        pltpu.make_async_copy(dual_hbm, gathered.at[0, me_row], small_sems.at[0]),
+        pltpu.make_async_copy(dual_hbm, gathered.at[me_row], small_sems.at[0]),
         pltpu.make_async_copy(offset_hbm, offset_ref, small_sems.at[1]),
         pltpu.make_async_copy(live_hbm, live_ref, small_sems.at[2]),
     ]
@@ -77,6 +77,8 @@
 
     column[rows:, :] = jnp.zeros((column.shape[0] - rows, LANES), jnp.float32)
     placing[...] = jnp.zeros(placing.shape, jnp.float32)
+    middle[:, :8, :] = jnp.zeros((n_row, 8, LANES), jnp.float32)
+    middle[:, 16:, :] = jnp.zeros((n_row, 8, LANES), jnp.float32)
     for copy in small:
         copy.wait()
     start = offset_ref[0]
@@ -86,6 +88,10 @@
     lane = lax.broadcasted_iota(jnp.int32, (8, LANES), 1)
     pl.semaphore_wait(barrier, others + len(shifts))
 
+    def wait_tiles(sem):
+        tiles = middle.at[pl.ds(0, others), pl.ds(8, 8)]
+        pltpu.make_async_copy(tiles, tiles, sem).wait()
+
     def row_peer(i):
         return lax.rem(me_row + i, n_row)
 
@@ -95,19 +101,27 @@
     def wait_others(ref, sem):
         pltpu.make_async_copy(ref.at[pl.ds(0, others)], ref.at[pl.ds(0, others)], sem).wait()
 
+    def cut_at(tile):
+        turned = pltpu.roll(tile, lax.rem(LANES - within, LANES), 1)
+        return jnp.where(lane < LANES - within, turned, pltpu.roll(turned, 7, 0))
+
+    for i in range(1, n_row):
+        pltpu.make_async_remote_copy(
+            src_ref=gathered.at[me_row], dst_ref=gathered.at[me_row],
+            send_sem=gather_send.at[0], recv_sem=gather_recv.at[0],
+            device_id=(row_peer(i), me_col), device_id_type=MESH).start()
+    for i in range(1, n_row):
+        pltpu.make_async_remote_copy(
+            src_ref=offset_ref, dst_ref=row_offsets.at[me_row],
+            send_sem=offset_send.at[0], recv_sem=offset_recv.at[0],
+            device_id=(row_peer(i), me_col), device_id_type=MESH).start()
+    wait_others(gathered, gather_recv.at[0])
+    for r in range(n_row):
+        column[r * part_rows:(r + 1) * part_rows, :] = gathered[r]
+    cut = cut_at(column[pl.ds(first, 8), :])
+
     pending = []
     for app in range(2):
-        for i in range(1, n_row):
-            pltpu.make_async_remote_copy(
-                src_ref=gathered.at[app, me_row], dst_ref=gathered.at[app, me_row],
-                send_sem=gather_send.at[app], recv_sem=gather_recv.at[app],
-                device_id=(row_peer(i), me_col), device_id_type=MESH).start()
-        wait_others(gathered.at[app], gather_recv.at[app])
-        for r in range(n_row):
-            column[r * part_rows:(r + 1) * part_rows, :] = gathered[app, r]
-        tile = column[pl.ds(first, 8), :]
-        turned = pltpu.roll(tile, lax.rem(LANES - within, LANES), 1)
-        cut = jnp.where(lane < LANES - within, turned, pltpu.roll(turned, 7, 0))
         cut_window[app] = cut
         windows, backs = [], []
         for h in range(hops):
@@ -141,25 +155,37 @@
             backs[h].wait_recv()
             total = total + back_in[app * hops + h]
         turned = pltpu.roll(total, within, 1)
-        placing[rows:rows + 8, :] = jnp.where(lane >= within, turned, pltpu.roll(turned, 1, 0))
-        for t in range(n_row):
-            outgoing[app, t] = placing[pl.ds(rows - first + t * part_rows, part_rows), :]
-        for i in range(1, n_row):
-            pltpu.make_async_remote_copy(
-                src_ref=outgoing.at[app, row_peer(i)], dst_ref=incoming.at[app, me_row],
-                send_sem=scatter_send.at[app], recv_sem=scatter_recv.at[app],
-                device_id=(row_peer(i), me_col), device_id_type=MESH).start()
-        incoming[app, me_row] = outgoing[app, me_row]
-        wait_others(incoming.at[app], scatter_recv.at[app])
-        summed = jnp.sum(incoming[app], axis=0)
+        total = jnp.where(lane >= within, turned, pltpu.roll(turned, 1, 0))
+        pending += windows + backs
         if app == 0:
-            gathered[1, me_row] = summed
-        else:
-            out_ref[...] = summed
-        pending += windows + backs
-    for app in range(2):
-        wait_others(gathered.at[app], gather_send.at[app])
-        wait_others(outgoing.at[app], scatter_send.at[app])
+            middle[me_row, 8:16, :] = total
+            for i in range(1, n_row):
+                pltpu.make_async_remote_copy(
+                    src_ref=middle.at[me_row, pl.ds(8, 8)], dst_ref=middle.at[me_row, pl.ds(8, 8)],
+                    send_sem=middle_send.at[0], recv_sem=middle_recv.at[0],
+                    device_id=(row_peer(i), me_col), device_id_type=MESH).start()
+            wait_others(row_offsets, offset_recv.at[0])
+            shifts = [jnp.clip(first - row_offsets[lax.rem(me_row + i, n_row), 0] // LANES, -8, 8) for i in range(1, n_row)]
+            wait_tiles(middle_recv.at[0])
+            tile = total
+            for i in range(1, n_row):
+                tile = tile + middle[lax.rem(me_row + i, n_row), pl.ds(8 + shifts[i - 1], 8), :]
+            cut = cut_at(tile)
+    placing[rows:rows + 8, :] = total
+    for t in range(n_row):
+        outgoing[t] = placing[pl.ds(rows - first + t * part_rows, part_rows), :]
+    for i in range(1, n_row):
+        pltpu.make_async_remote_copy(
+            src_ref=outgoing.at[row_peer(i)], dst_ref=incoming.at[me_row],
+            send_sem=scatter_send.at[0], recv_sem=scatter_recv.at[0],
+            device_id=(row_peer(i), me_col), device_id_type=MESH).start()
+    incoming[me_row] = outgoing[me_row]
+    wait_others(incoming, scatter_recv.at[0])
+    out_ref[...] = jnp.sum(incoming[...], axis=0)
+    wait_others(gathered, gather_send.at[0])
+    wait_others(row_offsets, offset_send.at[0])
+    wait_tiles(middle_send.at[0])
+    wait_others(outgoing, scatter_send.at[0])
     for copy in pending:
         copy.wait_send()
 
@@ -173,26 +199,29 @@
     depth, width = sub_basis.shape[1:]
     hbm = pl.BlockSpec(memory_space=pltpu.HBM)
     tiles = pltpu.VMEM((2 * hops, 8, LANES), jnp.float32)
-    parts = pltpu.VMEM((2, n_row, part_rows, LANES), jnp.float32)
+    parts = pltpu.VMEM((n_row, part_rows, LANES), jnp.float32)
     dma = pltpu.SemaphoreType.DMA
     out = pl.pallas_call(
         lambda *refs: kernel(n_row, n_col, hops, *refs),
-        out_shape=jax.ShapeDtypeStruct((part_rows, LANES), jnp.float32),
+        out_shape=pltpu.VMEM((part_rows, LANES), jnp.float32),
         in_specs=[hbm] * 5,
         out_specs=pl.BlockSpec(memory_space=pltpu.VMEM),
         scratch_shapes=[
             pltpu.VMEM((hops + 1, depth, width), jnp.bfloat16),
             parts,
             pltpu.VMEM((rows + 8, LANES), jnp.float32),
+            pltpu.VMEM((n_row, 24, LANES), jnp.float32),
+            pltpu.SMEM((n_row, 1), jnp.int32),
             pltpu.VMEM((2, 8, LANES), jnp.float32),
             tiles, tiles, tiles,
             pltpu.VMEM((2 * rows + 8, LANES), jnp.float32),
             parts, parts,
             pltpu.SMEM(pair_live.shape, jnp.int32),
             pltpu.SMEM(offsets.shape, jnp.int32),
-            dma((hops + 1,)), dma((3,)), dma((2,)), dma((2,)),
+            dma((hops + 1,)), dma((3,)), dma((1,)), dma((1,)),
+            dma((1,)), dma((1,)), dma((1,)), dma((1,)),
             dma((2 * hops,)), dma((2 * hops,)), dma((2 * hops,)), dma((2 * hops,)),
-            dma((2,)), dma((2,)),
+            dma((1,)), dma((1,)),
         ],
         compiler_params=pltpu.CompilerParams(
             collective_id=0, has_side_effects=True, vmem_limit_bytes=60 * 1024 * 1024),

time: 29.8 us -> 26.4 us (0.89)
  Pallas kernels: 27.7 us -> 25 us
  local copies, waits for them, and re-layouts: 1.26 us -> 0.58 us
    pallas_call x1, Pallas kernels: 27.7 us -> 25 us  [on_device(): pl.pallas_call(lambda *refs: kernel(n_row, n_col, hops, *refs), out_shape...]
    unnamed x1, local copies, waits for them, and re-layouts: 1.26 us -> 0.58 us
where the time goes in v4:
time: 26.4 us; the launch traced here: 26.2 us
  Pallas kernels  25 us (95%)
  between operations  0.66 us (2%)
  local copies, waits for them, and re-layouts  0.58 us (2%)
    pallas_call x1, Pallas kernels, on_device(): pl.pallas_call(lambda *refs: kernel(n_row, n_col, hops, *refs), out_shape...  25 us
    unnamed x1, local copies, waits for them, and re-layouts  0.58 us

profile of v4, /device:TPU:0, one launch (start us, length us, event | category | flops | bytes accessed | tf_op | source)
XLA Modules:
  0.0 26.2 jit_solution(8320687218679981405)
XLA Ops:
  0.7 25.0 %shard_map.55 = f32[4,128]{1,0:T(4,128)S(1)} custom-call(bf16[1,768,768]{2,1,0:T(8,128)(2,1)} %refs_0_.1, bf16[1,2,768,768]{3,2,1,0:T(8,128)(2,1)} %refs_1_.1, s32[1,2]{1,0:T(1,128)} %refs_2_.1, s32[1]{0:T(128)S(6)} %copy.8.refs_3_, f32[4,128]{1,0:T(4,128)} %bitcast.3), custom_call_target="tpu_custom_call" | custom-call | tf_op jit(solution)/shard_map/pallas_call | solution.py:204
  25.6 0.6 %copy.7 = f32[1,512]{1,0:T(1,128)} copy(f32[1,512]{1,0:T(1,128)S(1)} %bitcast.2) | data formatting | bytes 4096

commit v5 on v4

--- a/solution.py
+++ b/solution.py
@@ -48,7 +48,7 @@
 
 
 def kernel(n_row, n_col, hops, basis_hbm, coupling_hbm, live_hbm, offset_hbm, dual_hbm, out_ref,
-           mats, gathered, column, middle, row_offsets, cut_window, far_window, back_out, back_in, placing, outgoing, incoming,
+           mats, turned_basis, blocks, gathered, column, middle, row_offsets, cut_window, far_window, back_out, back_in, placing, outgoing, incoming,
            live_ref, offset_ref, load_sems, small_sems, gather_send, gather_recv,
            middle_send, middle_recv, offset_send, offset_recv, window_send, window_recv, back_send, back_recv, scatter_send, scatter_recv):
     me_row, me_col = lax.axis_index("row"), lax.axis_index("col")
@@ -65,7 +65,7 @@
     loads = [pltpu.make_async_copy(basis_hbm.at[0], mats.at[0], load_sems.at[0])]
     for h in range(hops):
         loads.append(pltpu.make_async_copy(coupling_hbm.at[0, h], mats.at[h + 1], load_sems.at[h + 1]))
-    for copy in small + loads:
+    for copy in small:
         copy.start()
 
     barrier = pltpu.get_barrier_semaphore()
@@ -75,6 +75,8 @@
     for shift in shifts:
         pl.semaphore_signal(barrier, inc=1, device_id=(me_row, lax.rem(me_col + shift, n_col)), device_id_type=MESH)
 
+    for load in loads:
+        load.start()
     column[rows:, :] = jnp.zeros((column.shape[0] - rows, LANES), jnp.float32)
     placing[...] = jnp.zeros(placing.shape, jnp.float32)
     middle[:, :8, :] = jnp.zeros((n_row, 8, LANES), jnp.float32)
@@ -115,6 +117,15 @@
             src_ref=offset_ref, dst_ref=row_offsets.at[me_row],
             send_sem=offset_send.at[0], recv_sem=offset_recv.at[0],
             device_id=(row_peer(i), me_col), device_id_type=MESH).start()
+    for load in loads:
+        load.wait()
+    turned_basis[...] = mats[0].T
+    step = min(256, blocks.shape[2])
+    for h in range(hops):
+        for n in range(0, blocks.shape[2], step):
+            blocks[h, :, n:n + step] = jnp.dot(
+                turned_basis[...], mats[h + 1, :, n:n + step],
+                preferred_element_type=jnp.float32).astype(jnp.bfloat16)
     wait_others(gathered, gather_recv.at[0])
     for r in range(n_row):
         column[r * part_rows:(r + 1) * part_rows, :] = gathered[r]
@@ -132,25 +143,23 @@
                 device_id=col_peer(-(h + 1)), device_id_type=MESH)
             copy.start()
             windows.append(copy)
-        if app == 0:
-            for load in loads:
-                load.wait()
-        projected = left_apply(mats[0], to_lanes(cut, chunks))
-        seen = split_rows(projected)
+        seen = split_rows(to_lanes(cut, chunks))
         for h in range(hops):
             slot = app * hops + h
-            back_out[slot] = lives[h] * to_tile(right_apply(seen, mats[h + 1]), chunks)
+            back_out[slot] = lives[h] * to_tile(right_apply(seen, blocks[h]), chunks)
             copy = pltpu.make_async_remote_copy(
                 src_ref=back_out.at[slot], dst_ref=back_in.at[slot],
                 send_sem=back_send.at[slot], recv_sem=back_recv.at[slot],
                 device_id=col_peer(h + 1), device_id_type=MESH)
             copy.start()
             backs.append(copy)
-        inner = projected
+        projected = right_apply(seen, turned_basis[...])
+        vector = right_apply(split_rows(projected), mats[0])
         for h in range(hops):
             windows[h].wait_recv()
-            inner = inner + lives[h] * left_apply(mats[h + 1], to_lanes(far_window[app * hops + h], chunks))
-        total = to_tile(right_apply(split_rows(inner), mats[0]), chunks)
+        for h in range(hops):
+            vector = vector + lives[h] * left_apply(blocks[h], to_lanes(far_window[app * hops + h], chunks))
+        total = to_tile(vector, chunks)
         for h in range(hops):
             backs[h].wait_recv()
             total = total + back_in[app * hops + h]
@@ -208,6 +217,8 @@
         out_specs=pl.BlockSpec(memory_space=pltpu.VMEM),
         scratch_shapes=[
             pltpu.VMEM((hops + 1, depth, width), jnp.bfloat16),
+            pltpu.VMEM((width, depth), jnp.bfloat16),
+            pltpu.VMEM((hops, width, width), jnp.bfloat16),
             parts,
             pltpu.VMEM((rows + 8, LANES), jnp.float32),
             pltpu.VMEM((n_row, 24, LANES), jnp.float32),

time: 26.4 us -> 25.6 us (0.970)
  Pallas kernels: 25 us -> 24.2 us
    pallas_call x1, Pallas kernels: 25 us -> 24.2 us  [on_device(): pl.pallas_call(lambda *refs: kernel(n_row, n_col, hops, *refs), out_shape...]
where the time goes in v5:
time: 25.6 us; the launch traced here: 25.5 us
  Pallas kernels  24.2 us (95%)
  between operations  0.66 us (3%)
  local copies, waits for them, and re-layouts  0.58 us (2%)
    pallas_call x1, Pallas kernels, on_device(): pl.pallas_call(lambda *refs: kernel(n_row, n_col, hops, *refs), out_shape...  24.2 us
    unnamed x1, local copies, waits for them, and re-layouts  0.58 us

profile of v5, /device:TPU:0, one launch (start us, length us, event | category | flops | bytes accessed | tf_op | source)
XLA Modules:
  0.0 25.5 jit_solution(13996828618059251488)
XLA Ops:
  0.7 24.2 %shard_map.55 = f32[4,128]{1,0:T(4,128)S(1)} custom-call(bf16[1,768,768]{2,1,0:T(8,128)(2,1)} %refs_0_.1, bf16[1,2,768,768]{3,2,1,0:T(8,128)(2,1)} %refs_1_.1, s32[1,2]{1,0:T(1,128)} %refs_2_.1, s32[1]{0:T(128)S(6)} %copy.8.refs_3_, f32[4,128]{1,0:T(4,128)} %bitcast.3), custom_call_target="tpu_custom_call" | custom-call | tf_op jit(solution)/shard_map/pallas_call | solution.py:213
  24.9 0.6 %copy.7 = f32[1,512]{1,0:T(1,128)} copy(f32[1,512]{1,0:T(1,128)S(1)} %bitcast.2) | data formatting | bytes 4096

commit v6 on v5

--- a/solution.py
+++ b/solution.py
@@ -23,11 +23,11 @@
     return jnp.broadcast_to(jnp.sum(products, axis=0, keepdims=True), products.shape)
 
 
-def left_apply(matrix, vector):
-    return spread(lax.dot_general(
+def left_products(matrix, vector):
+    return lax.dot_general(
         split_rows(vector), matrix, (((1,), (1,)), ((), ())),
         preferred_element_type=jnp.float32,
-    ))
+    )
 
 
 def right_apply(rows, matrix):
@@ -77,10 +77,6 @@
 
     for load in loads:
         load.start()
-    column[rows:, :] = jnp.zeros((column.shape[0] - rows, LANES), jnp.float32)
-    placing[...] = jnp.zeros(placing.shape, jnp.float32)
-    middle[:, :8, :] = jnp.zeros((n_row, 8, LANES), jnp.float32)
-    middle[:, 16:, :] = jnp.zeros((n_row, 8, LANES), jnp.float32)
     for copy in small:
         copy.wait()
     start = offset_ref[0]
@@ -112,6 +108,10 @@
             src_ref=gathered.at[me_row], dst_ref=gathered.at[me_row],
             send_sem=gather_send.at[0], recv_sem=gather_recv.at[0],
             device_id=(row_peer(i), me_col), device_id_type=MESH).start()
+    column[rows:, :] = jnp.zeros((column.shape[0] - rows, LANES), jnp.float32)
+    placing[...] = jnp.zeros(placing.shape, jnp.float32)
+    middle[:, :8, :] = jnp.zeros((n_row, 8, LANES), jnp.float32)
+    middle[:, 16:, :] = jnp.zeros((n_row, 8, LANES), jnp.float32)
     for i in range(1, n_row):
         pltpu.make_async_remote_copy(
             src_ref=offset_ref, dst_ref=row_offsets.at[me_row],
@@ -157,8 +157,8 @@
         vector = right_apply(split_rows(projected), mats[0])
         for h in range(hops):
             windows[h].wait_recv()
-        for h in range(hops):
-            vector = vector + lives[h] * left_apply(blocks[h], to_lanes(far_window[app * hops + h], chunks))
+        ahead = [lives[h] * left_products(blocks[h], to_lanes(far_window[app * hops + h], chunks)) for h in range(hops)]
+        vector = vector + spread(sum(ahead))
         total = to_tile(vector, chunks)
         for h in range(hops):
             backs[h].wait_recv()
@@ -181,13 +181,14 @@
                 tile = tile + middle[lax.rem(me_row + i, n_row), pl.ds(8 + shifts[i - 1], 8), :]
             cut = cut_at(tile)
     placing[rows:rows + 8, :] = total
-    for t in range(n_row):
-        outgoing[t] = placing[pl.ds(rows - first + t * part_rows, part_rows), :]
-    for i in range(1, n_row):
-        pltpu.make_async_remote_copy(
-            src_ref=outgoing.at[row_peer(i)], dst_ref=incoming.at[me_row],
-            send_sem=scatter_send.at[0], recv_sem=scatter_recv.at[0],
-            device_id=(row_peer(i), me_col), device_id_type=MESH).start()
+    for i in list(range(1, n_row)) + [0]:
+        peer = row_peer(i)
+        outgoing[peer] = placing[pl.ds(rows - first + peer * part_rows, part_rows), :]
+        if i > 0:
+            pltpu.make_async_remote_copy(
+                src_ref=outgoing.at[peer], dst_ref=incoming.at[me_row],
+                send_sem=scatter_send.at[0], recv_sem=scatter_recv.at[0],
+                device_id=(peer, me_col), device_id_type=MESH).start()
     incoming[me_row] = outgoing[me_row]
     wait_others(incoming, scatter_recv.at[0])
     out_ref[...] = jnp.sum(incoming[...], axis=0)

time: 25.6 us -> 25.6 us (level)
  no operation moved by 1% of the time
where the time goes in v6:
time: 25.6 us; the launch traced here: 25.5 us
  Pallas kernels  24.2 us (95%)
  between operations  0.66 us (3%)
  local copies, waits for them, and re-layouts  0.58 us (2%)
    pallas_call x1, Pallas kernels, on_device(): pl.pallas_call(lambda *refs: kernel(n_row, n_col, hops, *refs), out_shape...  24.2 us
    unnamed x1, local copies, waits for them, and re-layouts  0.58 us

profile of v6, /device:TPU:0, one launch (start us, length us, event | category | flops | bytes accessed | tf_op | source)
XLA Modules:
  0.0 25.5 jit_solution(18441886205307513610)
XLA Ops:
  0.7 24.2 %shard_map.55 = f32[4,128]{1,0:T(4,128)S(1)} custom-call(bf16[1,768,768]{2,1,0:T(8,128)(2,1)} %refs_0_.1, bf16[1,2,768,768]{3,2,1,0:T(8,128)(2,1)} %refs_1_.1, s32[1,2]{1,0:T(1,128)} %refs_2_.1, s32[1]{0:T(128)S(6)} %copy.8.refs_3_, f32[4,128]{1,0:T(4,128)} %bitcast.3), custom_call_target="tpu_custom_call" | custom-call | tf_op jit(solution)/shard_map/pallas_call | solution.py:214
  24.9 0.6 %copy.7 = f32[1,512]{1,0:T(1,128)} copy(f32[1,512]{1,0:T(1,128)S(1)} %bitcast.2) | data formatting | bytes 4096
